TPU v7x, 32 devices: a whole 2x2x4 slice. The times are simulated.
32 devices in a mesh: freq: 4 (over y, x), ma: 8 (over z, core).
Axes of the slice: x: 2, y: 2, z: 4, core: 2. Of those that a mesh axis runs over, the one named last changes fastest.
Arguments:
- sky_coeffs: bfloat16 [4, 2, 3, 256, 8, 16, 128], P('freq', None, None, None, 'ma'), may hold values from -6 to 6
- beam_transfer: bfloat16 [4, 8, 2, 3, 2048, 512], P('freq', 'ma'), may hold values from -0.078125 to 0.078125
- svd_basis: bfloat16 [4, 16, 2, 256, 512], P('freq', 'ma'), may hold values from -0.1875 to 0.1875
- kl_basis: bfloat16 [16, 2, 256, 4, 256], P('ma'), may hold values from -0.1875 to 0.1875
- m_values: int32 [16], P('ma'), may hold values from 1 to 2047, as said below
- svd_count: int32 [16], P('ma'), may hold values from 128 to 256, as said below
- kl_index: int32 [16, 128], P('ma'), may hold values from 0 to 255, as said below
- kl_count: int32 [16], P('ma'), may hold values from 64 to 128, as said below
Outputs:
- kl_modes: bfloat16 [16, 2, 128, 128], P('ma', None, None, 'freq')
Inputs may be any that keep to these rules, and one draw needn't show every extreme that they name: `m_values`: for each owner, the sum of 2048 - m over its 2 m-values is at most 2048, and equals 2048 for owner 0. `svd_count`: slot 0 retains all 256 modes. `kl_index`: entries of one m are distinct. `kl_count`: slot 0 retains all 128 modes.
All inputs are finite; a program needn't handle non-finite values.
Results may differ from a plain program's by a relative error of at most 0.012.
Values may be sent and summed in bfloat16 or wider, within the bound.
A program may use at most 128 MiB of HBM per device.

v0:
```python
import jax
import jax.numpy as jnp
from jax import lax
from jax.sharding import PartitionSpec as P


def pack_rows(sky_freq, m_owner):
    multipoles = sky_freq.shape[2]
    padded = jnp.pad(sky_freq, ((0, 0), (0, 0), (multipoles, multipoles), (0, 0), (0, 0)))
    row_index = jnp.arange(multipoles, dtype=jnp.int32)
    row_start = jnp.zeros((), jnp.int32)
    packed_list = []
    for slot_num in range(sky_freq.shape[3]):
        span_len = multipoles - m_owner[slot_num]
        row_shift = m_owner[slot_num] - row_start
        shifted = lax.dynamic_slice_in_dim(
            padded[:, :, :, slot_num, :], multipoles + row_shift, multipoles, 2
        )
        row_mask = (row_index >= row_start) & (row_index < row_start + span_len)
        packed_list.append(
            jnp.where(row_mask[None, None, :, None], shifted, jnp.zeros((), shifted.dtype))
        )
        row_start = row_start + span_len
    return jnp.stack(packed_list, 3)


def complex_stack(first_part, second_part):
    return jnp.stack([jnp.stack([first_part, -second_part]), jnp.stack([second_part, first_part])])


def shards(sky_coeffs, beam_transfer, svd_basis, kl_basis, m_values, svd_count, kl_index, kl_count):
    beam_owner = beam_transfer[0, 0]
    svd_owner = svd_basis[0]
    mode_total = svd_owner.shape[2]
    whole = lax.all_to_all(sky_coeffs, "ma", split_axis=5, concat_axis=4, tiled=True)[0]
    merged = whole.reshape(
        2, whole.shape[1], whole.shape[2] * whole.shape[3], whole.shape[4], whole.shape[5]
    )
    packed = pack_rows(merged, m_values)
    stacked = complex_stack(packed[0], packed[1])
    visibility = lax.dot_general(
        stacked, beam_owner, (((1, 2, 3), (0, 1, 2)), ((), ())), preferred_element_type=jnp.float32
    ).astype(jnp.bfloat16)
    rotated = jnp.stack(
        [jnp.stack([visibility[0], visibility[1]]), jnp.stack([visibility[1], -visibility[0]])]
    )
    coefficients = jnp.einsum(
        "oqsrb,sqjb->osjr", rotated, svd_owner, preferred_element_type=jnp.float32
    )
    mode_mask = jnp.arange(mode_total, dtype=jnp.int32)[None, :] < svd_count[:, None]
    coefficients = jnp.where(mode_mask[None, :, :, None], coefficients, 0.0).astype(jnp.bfloat16)
    selected = jax.vmap(lambda basis_one, chosen: jnp.take(basis_one, chosen, axis=1))(
        kl_basis, kl_index
    )
    keep_mask = jnp.arange(selected.shape[2], dtype=jnp.int32)[None, :] < kl_count[:, None]
    spread = lax.all_to_all(
        coefficients[:, :, None], "freq", split_axis=4, concat_axis=2, tiled=True
    )
    stacked = complex_stack(spread[0], spread[1])
    kl_out = jnp.einsum("oqsfjr,sqifj->soir", stacked, selected, preferred_element_type=jnp.float32)
    kl_out = jnp.where(keep_mask[:, None, :, None], kl_out, 0.0)
    return kl_out.astype(jnp.bfloat16)


def solution(mesh):
    return jax.shard_map(
        shards,
        mesh=mesh,
        in_specs=(
            P("freq", None, None, None, "ma", None, None),
            P("freq", "ma", None, None, None, None),
            P("freq", "ma", None, None, None),
            P("ma", None, None, None, None),
            P("ma"),
            P("ma"),
            P("ma", None),
            P("ma"),
        ),
        out_specs=P("ma", None, None, "freq"),
        check_vma=False,
    )
```

profile of v0, /device:TPU:0, one launch (start us, length us, event | category | flops | bytes accessed | tf_op | source)
XLA Modules:
  0.0 216.5 jit_solution(16721079827278895955)
XLA Ops:
  0.0 0.0 copy-start
  0.0 7.2 %copy.20 = bf16[1,2,3,256,1,16,128]{6,3,2,1,4,0,5:T(8,128)(2,1)} copy(bf16[1,2,3,256,1,16,128]{6,5,4,3,2,1,0:T(8,128)(2,1)} %param.8) | data formatting | bytes 12582912 | tf_op args[0]
  7.2 0.0 copy-start.4
  7.2 0.0 copy-start.3
  7.2 0.0 copy-start.7
  7.2 6.5 %all-to-all-start = ((bf16[1,2,3,256,1,16,128]{6,3,2,1,4,0,5:T(8,128)(2,1)}), bf16[1,2,3,256,1,16,128]{6,3,2,1,4,0,5:T(8,128)(2,1)}, u32[]{:S(2)}, u32[]{:S(2)}) async-start(bf16[1,2,3,256,1,16,128]{6,3,2,1,4,0,5:T(8,128)(2,1)} %copy.20), calls=%async_computation | async-start | bytes 12582912 | tf_op jit(solution)/shard_map/all_to_all | solution.py:35
  13.7 0.0 copy-done.4
  13.7 0.6 fusion.38
  17.3 0.0 copy-done.3
  17.3 0.0 copy-done
  17.3 2.9 %gather_fusion = bf16[256,2,4,256]{3,2,1,0:T(4,128)(2,1)} fusion(bf16[2,2,256,4,256]{4,3,2,1,0:T(4,128)(2,1)S(1)} %copy-done, s32[256]{0:T(256)S(1)} %fusion.31), kind=kCustom, calls=%fused_computation | custom fusion | bytes 2099200 | tf_op jit(solution)/shard_map/vmap(jit(_take))/gather | solution.py:52
  20.2 0.0 copy-done.7
  20.3 0.1 iota_compare_fusion.3
  20.3 132.4 %all-to-all-done = bf16[1,2,3,256,1,16,128]{6,3,2,1,4,0,5:T(8,128)(2,1)} async-done(((bf16[1,2,3,256,1,16,128]{6,3,2,1,4,0,5:T(8,128)(2,1)}), bf16[1,2,3,256,1,16,128]{6,3,2,1,4,0,5:T(8,128)(2,1)}, u32[]{:S(2)}, u32[]{:S(2)}) %all-to-all-start) | async-done | bytes 6291488 | tf_op jit(solution)/shard_map/all_to_all | solution.py:35
  152.7 9.5 %copy.21 = bf16[1,2,3,256,1,16,128]{6,5,3,2,1,4,0:T(8,128)(2,1)} copy(bf16[1,2,3,256,1,16,128]{6,3,2,1,4,0,5:T(8,128)(2,1)} %all-to-all-done) | data formatting | bytes 12582912 | tf_op jit(solution)/shard_map/all_to_all | solution.py:35
  162.2 16.3 %copy.22 = bf16[2,3,2048,2,128]{2,4,1,0,3:T(8,128)(2,1)} copy(bf16[2,3,2048,2,128]{4,3,2,1,0:T(2,128)(2,1)} %bitcast.89) | data formatting | bytes 12582912 | tf_op jit(solution)/shard_map/reshape;squeeze | solution.py:36
  178.5 4.6 %pad_slice_fusion = (bf16[2,3,6144,1,128]{2,4,1,0,3:T(8,128)(2,1)S(1)}, bf16[2,3,6144,1,128]{2,4,1,0,3:T(8,128)(2,1)S(1)}) fusion(bf16[2,3,2048,2,128]{2,4,1,0,3:T(8,128)(2,1)} %copy.22), kind=kLoop, calls=%fused_computation.1 | loop fusion | bytes 25165824 | tf_op jit(solution)/shard_map/slice | solution.py:17
  183.1 6.4 %dynamic-slice_select_fusion = (bf16[2,3,2048,1,128]{2,4,1,0,3:T(8,128)(2,1)S(1)}, bf16[2,3,2048,1,128]{2,4,1,0,3:T(8,128)(2,1)}) fusion(bf16[2,3,6144,1,128]{2,4,1,0,3:T(8,128)(2,1)S(1)} %get-tuple-element.8, s32[]{:T(128)S(6)} %select_n.38, pred[2048]{0:T(1024)(128)(4,1)S(1)} %fusion.30, bf16[2,3,6144,1,128]{2,4,1,0,3:T(8,128)(2,1)S(1)} %get-tuple-element.9, ...), kind=kLoop, calls=%fused_computation.14 | loop fusion | flops 3145728 | bytes 12587016 | tf_op jit(solution)/shard_map/jit(_where)/select_n | solution.py:21
  189.5 2.2 %fusion.36 = (bf16[1,3,2048,2,128]{2,4,1,0,3:T(8,128)(2,1)S(1)}, bf16[1,3,2048,2,128]{2,4,1,0,3:T(8,128)(2,1)S(1)}, bf16[1,3,2048,2,128]{2,4,1,0,3:T(8,128)(2,1)S(1)}) fusion(bf16[2,3,2048,1,128]{2,4,1,0,3:T(8,128)(2,1)S(1)} %get-tuple-element.20, bf16[2,3,2048,1,128]{2,4,1,0,3:T(8,128)(2,1)} %get-tuple-element.21), kind=kLoop, calls=%fused_computation.56 | loop fusion | flops 4718592 | bytes 15728640 | tf_op jit(solution)/shard_map/neg | solution.py:28
  191.7 1.3 maximum_bitcast_fusion
  193.0 0.0 copy-start.6
  193.0 0.0 copy-start.1
  193.0 11.4 %fusion.11 = bf16[2,2,128,512]{3,2,1,0:T(8,128)(2,1)S(1)} fusion(bf16[1,1,2,3,2048,512]{5,4,3,2,1,0:T(8,128)(2,1)} %param.9, bf16[1,2,3,2048,2,128]{3,5,2,1,4,0:T(8,128)(2,1)S(1)} %get-tuple-element.11, bf16[1,2,3,2048,2,128]{3,5,2,1,4,0:T(8,128)(2,1)S(1)} %get-tuple-element.10), kind=kOutput, calls=%fused_computation.17 | convolution fusion | flops 6449004544 | bytes 25690112 | tf_op jit(solution)/shard_map/dot_general | solution.py:41
  204.4 0.0 copy-start.5
  204.4 0.0 copy-start.2
  204.5 0.1 maximum_bitcast_fusion.2
  204.5 0.0 copy-done.6
  204.5 0.5 fusion.18
  205.0 1.0 copy.24
  206.0 3.7 %all-to-all-start.1 = ((bf16[2,2,1,256,128]{3,0,1,2,4:T(2,128)(2,1)}), bf16[2,2,1,256,128]{3,0,1,2,4:T(2,128)(2,1)S(1)}, u32[]{:S(2)}, u32[]{:S(2)}) async-start(bf16[2,2,1,256,128]{3,0,1,2,4:T(2,128)(2,1)} %copy.24), calls=%async_computation.1 | async-start | bytes 524288 | tf_op jit(solution)/shard_map/all_to_all | solution.py:56
  209.7 0.0 copy-done.5
  209.7 0.1 compare_and_fusion
  209.8 5.3 %all-to-all-done.1 = bf16[2,2,1,256,128]{3,0,1,2,4:T(2,128)(2,1)S(1)} async-done(((bf16[2,2,1,256,128]{3,0,1,2,4:T(2,128)(2,1)}), bf16[2,2,1,256,128]{3,0,1,2,4:T(2,128)(2,1)S(1)}, u32[]{:S(2)}, u32[]{:S(2)}) %all-to-all-start.1) | async-done | bytes 262176 | tf_op jit(solution)/shard_map/all_to_all | solution.py:56
  215.2 0.0 copy-done.2
  215.2 1.3 fusion.21
  216.5 0.0 copy-done.1
  (8 shorter events, 0.2 us)
Async XLA Ops:
  0.0 17.3 %copy-start = (bf16[2,2,256,4,256]{4,3,2,1,0:T(4,128)(2,1)S(1)}, bf16[2,2,256,4,256]{4,3,2,1,0:T(4,128)(2,1)}, u32[]{:S(2)}) copy-start(bf16[2,2,256,4,256]{4,3,2,1,0:T(4,128)(2,1)} %param.11) | copy-start | bytes 6291460
  7.2 6.5 %copy-start.4 = (s32[2]{0:T(128)S(1)}, s32[2]{0:T(128)}, u32[]{:S(2)}) copy-start(s32[2]{0:T(128)} %param.12) | copy-start | bytes 28
  7.2 10.1 %copy-start.3 = (s32[2,128]{1,0:T(2,128)S(1)}, s32[2,128]{1,0:T(2,128)}, u32[]{:S(2)}) copy-start(s32[2,128]{1,0:T(2,128)} %param.14) | copy-start | bytes 3076
  7.2 13.0 %copy-start.7 = (s32[2]{0:T(128)S(1)}, s32[2]{0:T(128)}, u32[]{:S(2)}) copy-start(s32[2]{0:T(128)} %param.13) | copy-start | bytes 28
  7.2 145.5 %all-to-all-start = ((bf16[1,2,3,256,1,16,128]{6,3,2,1,4,0,5:T(8,128)(2,1)}), bf16[1,2,3,256,1,16,128]{6,3,2,1,4,0,5:T(8,128)(2,1)}, u32[]{:S(2)}, u32[]{:S(2)}) async-start(bf16[1,2,3,256,1,16,128]{6,3,2,1,4,0,5:T(8,128)(2,1)} %copy.20), calls=%async_computation | async-start | bytes 12582912 | tf_op jit(solution)/shard_map/all_to_all | solution.py:35
  193.0 11.5 %copy-start.6 = (bf16[1,2,2,256,512]{4,3,2,1,0:T(8,128)(2,1)S(1)}, bf16[1,2,2,256,512]{4,3,2,1,0:T(8,128)(2,1)}, u32[]{:S(2)}) copy-start(bf16[1,2,2,256,512]{4,3,2,1,0:T(8,128)(2,1)} %param.10) | copy-start | bytes 3145732
  193.0 23.5 %copy-start.1 = (bf16[2,2,256,4,256]{4,3,2,1,0:T(4,128)(2,1)S(1)}, bf16[2,2,256,4,256]{4,3,2,1,0:T(4,128)(2,1)}, u32[]{:S(2)}) copy-start(bf16[2,2,256,4,256]{4,3,2,1,0:T(4,128)(2,1)} %param.11) | copy-start | bytes 6291460
  204.4 5.3 %copy-start.5 = (s32[2]{0:T(128)S(1)}, s32[2]{0:T(128)}, u32[]{:S(2)}) copy-start(s32[2]{0:T(128)} %param.15) | copy-start | bytes 28
  204.4 10.8 %copy-start.2 = (bf16[256,2,4,256]{3,2,1,0:T(4,128)(2,1)S(1)}, bf16[256,2,4,256]{3,2,1,0:T(4,128)(2,1)}, u32[]{:S(2)}) copy-start(bf16[256,2,4,256]{3,2,1,0:T(4,128)(2,1)} %gather_fusion) | copy-start | bytes 3145732
  206.0 9.1 %all-to-all-start.1 = ((bf16[2,2,1,256,128]{3,0,1,2,4:T(2,128)(2,1)}), bf16[2,2,1,256,128]{3,0,1,2,4:T(2,128)(2,1)S(1)}, u32[]{:S(2)}, u32[]{:S(2)}) async-start(bf16[2,2,1,256,128]{3,0,1,2,4:T(2,128)(2,1)} %copy.24), calls=%async_computation.1 | async-start | bytes 524288 | tf_op jit(solution)/shard_map/all_to_all | solution.py:56
where the time goes:
time: 217 us; the launch traced here: 216 us
  waiting for transfers between devices  138 us (64%)
  local copies, waits for them, and re-layouts  42.1 us (19%)
  matrix products  13.1 us (6%)
  starting transfers between devices  10.2 us (5%)
  other arithmetic  10.2 us (5%)
  between operations  3.21 us (1%)
    all_to_all x1, waiting for transfers between devices, shards(): lax.all_to_all(sky_coeffs, 'ma', split_axis=5, concat_axis=4, tiled=True)[0]  132 us
    another operation x1, local copies, waits for them, and re-layouts, shards(): whole.reshape(2, whole.shape[1], whole.shape[2] * whole.shape[3], whole.s...  16.3 us
    dot_general x1, matrix products, shards(): lax.dot_general(stacked, beam_owner, (((1, 2, 3), (0, 1, 2)), ((), ())),...  11.4 us
    all_to_all x1, local copies, waits for them, and re-layouts, shards(): lax.all_to_all(sky_coeffs, 'ma', split_axis=5, concat_axis=4, tiled=True)[0]  9.45 us
    unnamed x17, local copies, waits for them, and re-layouts  7.23 us
    all_to_all x1, starting transfers between devices, shards(): lax.all_to_all(sky_coeffs, 'ma', split_axis=5, concat_axis=4, tiled=True)[0]  6.49 us
    select_n x1, other arithmetic, pack_rows(): jnp.where(row_mask[None, None, :, None], shifted, jnp.zeros((), shifted.d...  6.39 us
    all_to_all x1, waiting for transfers between devices, shards(): lax.all_to_all(coefficients[:, :, None], 'freq', split_axis=4, concat_axi...  5.3 us
  transfers between devices with their start and end apart: 2, of which 2 were waited for; matrix products, arithmetic and copies ran while one was open for 2% of the time, Pallas kernels for 0%

commit v1 on v0

v1 whole, which is shorter than its diff:
```python
import functools

import jax
import jax.numpy as jnp
from jax import lax
from jax.experimental import pallas as pl
from jax.experimental.pallas import tpu as pltpu
from jax.sharding import PartitionSpec as P

MESH = pl.DeviceIdType.MESH
F32 = jnp.float32
BF16 = jnp.bfloat16


def partner(me, step, size):
    out, bit = 0, 1
    while bit < size:
        a, b = (me // bit) % 2, (step // bit) % 2
        out = out + bit * (a + b - 2 * a * b)
        bit *= 2
    return out


def exchange_kernel(
    lanes, rows, slots, block, kblock,
    m_ref, sky_ref, beam_ref, vis_ref,
    m_all, m_smem, sky_buf, wide, send, recv, extra_send, extra_recv, beam_buf,
    stage, mixed, turned, acc_r, acc_i,
    m_send, m_recv, m_local, sky_sem, beam_sem, send_sem, recv_sem, ex_send, ex_recv,
):
    me = lax.axis_index("ma")
    chunks = sky_ref.shape[0]
    pols = chunks // 2
    total = lanes * rows
    reals = sky_ref.shape[2]

    for ch in range(chunks):
        pltpu.make_async_copy(sky_ref.at[ch], sky_buf.at[ch], sky_sem.at[ch]).start()
    for part in range(2):
        for pol in range(pols):
            pltpu.make_async_copy(
                beam_ref.at[part, pol], beam_buf.at[part, pol], beam_sem.at[part, pol]
            ).start()

    barrier = pltpu.get_barrier_semaphore()

    @pl.loop(1, lanes)
    def _(step):
        pl.semaphore_signal(
            barrier, inc=1, device_id={"ma": partner(me, step, lanes)}, device_id_type=MESH
        )

    pl.semaphore_wait(barrier, lanes - 1)

    def m_copy(step):
        peer = partner(me, step, lanes)
        return pltpu.make_async_remote_copy(
            src_ref=m_ref, dst_ref=m_all.at[me], send_sem=m_send.at[peer],
            recv_sem=m_recv.at[me], device_id={"ma": peer}, device_id_type=MESH,
        )

    def m_arrival(step):
        peer = partner(me, step, lanes)
        return pltpu.make_async_remote_copy(
            src_ref=m_ref, dst_ref=m_all.at[peer], send_sem=m_send.at[peer],
            recv_sem=m_recv.at[peer], device_id={"ma": peer}, device_id_type=MESH,
        )

    @pl.loop(0, lanes - 1)
    def _(i):
        m_copy(lanes - 1 - i).start()

    m_all[me] = m_ref[...]

    def widen(ch):
        pltpu.make_async_copy(sky_ref.at[ch], sky_buf.at[ch], sky_sem.at[ch]).wait()
        piece = 256

        @pl.loop(0, rows * slots // piece)
        def _(i):
            at = pl.multiple_of(i * piece, piece)
            wide[ch, pl.ds(at, piece), :] = sky_buf[ch, pl.ds(at, piece), :].astype(F32)

        wide[ch, pl.ds(rows * slots, block * slots), :] = jnp.zeros((block * slots, reals), F32)

    widen(0)

    @pl.loop(1, lanes)
    def _(step):
        copy = m_arrival(step)
        copy.wait_recv()
        copy.wait_send()

    local = pltpu.make_async_copy(m_all, m_smem, m_local)
    local.start()
    local.wait()

    row_in_block = lax.broadcasted_iota(jnp.int32, (block, reals), 0)

    def pack(ch):
        @pl.loop(0, lanes)
        def _(owner):
            m0, m1 = m_smem[owner, 0, 0], m_smem[owner, 1, 0]
            start1 = total - m0
            excess = m0 + m1 - total
            first0 = (m0 - me + lanes - 1) // lanes
            first1 = (excess - me + lanes - 1) // lanes
            residue = lanes * first0 + me - m0

            @pl.loop(0, rows // block)
            def _(i):
                k0 = i * block
                r0 = jnp.clip(first0 + k0, 0, rows)
                r1 = jnp.clip(first1 + k0, 0, rows)
                v0 = wide[ch, pl.ds(r0 * slots + 2 * owner, block, stride=slots), :]
                v1 = wide[ch, pl.ds(r1 * slots + 2 * owner + 1, block, stride=slots), :]
                packed_at = lanes * (row_in_block + k0) + residue
                value = jnp.where(packed_at < start1, v0, v1).astype(BF16)
                send[ch, owner, pl.ds(pl.multiple_of(k0, block), block), :] = value

        recv[ch, me] = send[ch, me]

    def slab(ch, peer, sender):
        return pltpu.make_async_remote_copy(
            src_ref=send.at[ch, peer], dst_ref=recv.at[ch, sender],
            send_sem=send_sem.at[ch, peer], recv_sem=recv_sem.at[ch, sender],
            device_id={"ma": peer}, device_id_type=MESH,
        )

    def extra_slab(peer, sender):
        return pltpu.make_async_remote_copy(
            src_ref=extra_send.at[peer], dst_ref=extra_recv.at[sender],
            send_sem=ex_send.at[peer], recv_sem=ex_recv.at[sender],
            device_id={"ma": peer}, device_id_type=MESH,
        )

    def ship(ch):
        @pl.loop(0, lanes - 1)
        def _(i):
            slab(ch, partner(me, lanes - 1 - i, lanes), me).start()

    pack(0)
    ship(0)
    for ch in range(1, chunks):
        widen(ch)

    tile = lax.broadcasted_iota(jnp.int32, (16, reals), 0)

    @pl.loop(0, lanes)
    def _(owner):
        m0, m1 = m_smem[owner, 0, 0], m_smem[owner, 1, 0]
        start1 = total - m0
        first1 = (m0 + m1 - total - me + lanes - 1) // lanes
        row = jnp.clip(start1 // lanes + first1, 0, rows)
        value = jnp.zeros((16, reals), F32)
        for ch in range(chunks):
            one = wide[ch, pl.ds(row * slots + 2 * owner + 1, 1), :]
            value = jnp.where(tile == ch, one, value)
        extra_send[owner] = value.astype(BF16)

    extra_recv[me] = extra_send[me]

    @pl.loop(0, lanes - 1)
    def _(i):
        extra_slab(partner(me, lanes - 1 - i, lanes), me).start()

    @pl.loop(1, chunks)
    def _(ch):
        pack(ch)
        ship(ch)

    acc_r[...] = jnp.zeros_like(acc_r)
    acc_i[...] = jnp.zeros_like(acc_i)
    my0, my1 = m_smem[me, 0, 0], m_smem[me, 1, 0]
    start1 = total - my0
    end1 = start1 + total - my1
    q = start1 // lanes

    for part in range(2):
        for pol in range(pols):
            pltpu.make_async_copy(
                beam_ref.at[part, pol], beam_buf.at[part, pol], beam_sem.at[part, pol]
            ).wait()

    @pl.loop(1, lanes)
    def _(step):
        peer = partner(me, step, lanes)
        extra_slab(peer, peer).wait_recv()
        extra_slab(peer, peer).wait_send()

    @pl.loop(0, chunks)
    def _(ch):
        @pl.loop(1, lanes)
        def _(step):
            peer = partner(me, step, lanes)
            slab(ch, peer, peer).wait_recv()
            slab(ch, peer, peer).wait_send()

        @pl.loop(0, lanes)
        def _(lane):
            stage[lane] = recv[ch, lane].astype(F32)

        @pl.loop(0, lanes)
        def _(residue):
            lane0 = (residue + my0) % lanes
            lane1 = (residue + my0 + my1) % lanes
            spare_all = extra_recv[lane1].astype(F32)
            spare = jnp.sum(jnp.where(tile == ch, spare_all, 0.0), axis=0, keepdims=True)

            @pl.loop(0, rows // block)
            def _(i):
                k0 = pl.multiple_of(i * block, block)
                v0 = stage[lane0, pl.ds(k0, block), :]
                v1 = stage[lane1, pl.ds(k0, block), :]
                k = row_in_block + k0
                at = lanes * k + residue
                v1 = jnp.where(k == q, spare, v1)
                v1 = jnp.where(at < end1, v1, 0.0)
                mixed[pl.ds(residue + lanes * k0, block, stride=lanes), :] = jnp.where(
                    at < start1, v0, v1
                )

        part = ch // pols
        pol = ch % pols
        sign = (1 - 2 * part).astype(F32)

        @pl.loop(0, total // kblock)
        def _(i):
            at = pl.multiple_of(i * kblock, kblock)
            flat = mixed[pl.ds(at, kblock), :].T
            place = lax.broadcasted_iota(jnp.int32, (reals, kblock), 1) + at
            turned[pl.ds(0, reals), :] = jnp.where(place < start1, flat, 0.0).astype(BF16)
            turned[pl.ds(reals, reals), :] = jnp.where(place < start1, 0.0, flat).astype(BF16)
            both = turned[...]
            acc_r[...] += sign * jnp.dot(
                both, beam_buf[part, pol, pl.ds(at, kblock), :], preferred_element_type=F32
            )
            acc_i[...] += jnp.dot(
                both, beam_buf[1 - part, pol, pl.ds(at, kblock), :], preferred_element_type=F32
            )

    vis_ref[0] = acc_r[...].astype(BF16)
    vis_ref[1] = acc_i[...].astype(BF16)


def exchange(sky, beam, m_values):
    lanes = lax.axis_size("ma")
    parts, pols, rows, slots, reals = sky.shape
    total, bases = beam.shape[2], beam.shape[3]
    chunks = parts * pols
    block, kblock = 32, 512
    m_tile = jnp.zeros((8, 128), jnp.int32).at[:2].set(
        jnp.broadcast_to(m_values[:, None], (2, 128))
    )
    flat = sky.reshape(chunks, rows * slots, reals)
    any_space = pl.BlockSpec(memory_space=pl.ANY)
    vmem = pl.BlockSpec(memory_space=pltpu.VMEM)
    dma = pltpu.SemaphoreType.DMA
    return pl.pallas_call(
        functools.partial(exchange_kernel, lanes, rows, slots, block, kblock),
        out_shape=jax.ShapeDtypeStruct((2, 2 * reals, bases), BF16),
        in_specs=[vmem, any_space, any_space],
        out_specs=vmem,
        scratch_shapes=[
            pltpu.VMEM((lanes, 8, 128), jnp.int32),
            pltpu.SMEM((lanes, 8, 128), jnp.int32),
            pltpu.VMEM((chunks, rows * slots, reals), BF16),
            pltpu.VMEM((chunks, (rows + block) * slots, reals), F32),
            pltpu.VMEM((chunks, lanes, rows, reals), BF16),
            pltpu.VMEM((chunks, lanes, rows, reals), BF16),
            pltpu.VMEM((lanes, 16, reals), BF16),
            pltpu.VMEM((lanes, 16, reals), BF16),
            pltpu.VMEM((2, pols, total, bases), BF16),
            pltpu.VMEM((lanes, rows, reals), F32),
            pltpu.VMEM((total, reals), F32),
            pltpu.VMEM((2 * reals, kblock), BF16),
            pltpu.VMEM((2 * reals, bases), F32),
            pltpu.VMEM((2 * reals, bases), F32),
            dma((lanes,)), dma((lanes,)), dma,
            dma((chunks,)), dma((2, pols)),
            dma((chunks, lanes)), dma((chunks, lanes)), dma((lanes,)), dma((lanes,)),
        ],
        compiler_params=pltpu.CompilerParams(
            collective_id=0, has_side_effects=True, vmem_limit_bytes=64_000_000
        ),
    )(m_tile, flat, beam)


def complex_stack(first_part, second_part):
    return jnp.stack([jnp.stack([first_part, -second_part]), jnp.stack([second_part, first_part])])


def shards(sky_coeffs, beam_transfer, svd_basis, kl_basis, m_values, svd_count, kl_index, kl_count):
    svd_owner = svd_basis[0]
    mode_total = svd_owner.shape[2]
    reals = sky_coeffs.shape[-1]
    selected = jax.vmap(lambda basis_one, chosen: jnp.take(basis_one, chosen, axis=1))(
        kl_basis, kl_index
    )
    visibility = exchange(sky_coeffs[0, :, :, :, 0], beam_transfer[0, 0], m_values)
    visibility = visibility.reshape(2, 2, reals, visibility.shape[-1])
    rotated = jnp.stack(
        [jnp.stack([visibility[0], visibility[1]]), jnp.stack([visibility[1], -visibility[0]])]
    )
    coefficients = jnp.einsum(
        "oqsrb,sqjb->osjr", rotated, svd_owner, preferred_element_type=jnp.float32
    )
    mode_mask = jnp.arange(mode_total, dtype=jnp.int32)[None, :] < svd_count[:, None]
    coefficients = jnp.where(mode_mask[None, :, :, None], coefficients, 0.0).astype(jnp.bfloat16)
    keep_mask = jnp.arange(selected.shape[2], dtype=jnp.int32)[None, :] < kl_count[:, None]
    spread = lax.all_to_all(
        coefficients[:, :, None], "freq", split_axis=4, concat_axis=2, tiled=True
    )
    stacked = complex_stack(spread[0], spread[1])
    kl_out = jnp.einsum("oqsfjr,sqifj->soir", stacked, selected, preferred_element_type=jnp.float32)
    kl_out = jnp.where(keep_mask[:, None, :, None], kl_out, 0.0)
    return kl_out.astype(jnp.bfloat16)


def solution(mesh):
    return jax.shard_map(
        shards,
        mesh=mesh,
        in_specs=(
            P("freq", None, None, None, "ma", None, None),
            P("freq", "ma", None, None, None, None),
            P("freq", "ma", None, None, None),
            P("ma", None, None, None, None),
            P("ma"),
            P("ma"),
            P("ma", None),
            P("ma"),
        ),
        out_specs=P("ma", None, None, "freq"),
        check_vma=False,
    )
```

time: 217 us -> 103 us (0.47)
  waiting for transfers between devices: 138 us -> 3.33 us
  Pallas kernels: 0 us -> 86.6 us
  local copies, waits for them, and re-layouts: 42.1 us -> 5.54 us
  matrix products: 13.1 us -> 2.97 us
  other arithmetic: 10.2 us -> 0.33 us
  starting transfers between devices: 10.2 us -> 3.72 us
  between operations: 3.21 us -> 0.11 us
    all_to_all x1 -> x0, waiting for transfers between devices: 132 us -> none  [shards(): lax.all_to_all(sky_coeffs, 'ma', split_axis=5, concat_axis=4, tiled=True)[0]]
    pallas_call x0 -> x1, Pallas kernels: none -> 86.6 us  [exchange(): pl.pallas_call(functools.partial(exchange_kernel, lanes, rows, slots, blo...]
    another operation x1 -> x0, local copies, waits for them, and re-layouts: 16.3 us -> none  [shards(): whole.reshape(2, whole.shape[1], whole.shape[2] * whole.shape[3], whole.s...]
    dot_general x1 -> x0, matrix products: 11.4 us -> none  [shards(): lax.dot_general(stacked, beam_owner, (((1, 2, 3), (0, 1, 2)), ((), ())),...]
    all_to_all x1 -> x0, local copies, waits for them, and re-layouts: 9.45 us -> none  [shards(): lax.all_to_all(sky_coeffs, 'ma', split_axis=5, concat_axis=4, tiled=True)[0]]
    unnamed x17 -> x8, local copies, waits for them, and re-layouts: 7.23 us -> 0.02 us
    all_to_all x1 -> x0, starting transfers between devices: 6.49 us -> none  [shards(): lax.all_to_all(sky_coeffs, 'ma', split_axis=5, concat_axis=4, tiled=True)[0]]
    select_n x1 -> x0, other arithmetic: 6.39 us -> none  [pack_rows(): jnp.where(row_mask[None, None, :, None], shifted, jnp.zeros((), shifted.d...]
  transfers between devices with their start and end apart: 2 -> 1, of which waited for: 2 -> 1; matrix products, arithmetic and copies ran while one was open for 2% -> 2% of each run, Pallas kernels for 0% -> 0%
where the time goes in v1:
time: 103 us
  Pallas kernels  86.6 us (84%)
  local copies, waits for them, and re-layouts  5.54 us (5%)
  starting transfers between devices  3.72 us (4%)
  waiting for transfers between devices  3.33 us (3%)
  matrix products  2.97 us (3%)
    pallas_call x1, Pallas kernels, exchange(): pl.pallas_call(functools.partial(exchange_kernel, lanes, rows, slots, blo...  86.6 us
    all_to_all x1, starting transfers between devices, shards(): lax.all_to_all(coefficients[:, :, None], 'freq', split_axis=4, concat_axi...  3.72 us
    all_to_all x1, waiting for transfers between devices, shards(): lax.all_to_all(coefficients[:, :, None], 'freq', split_axis=4, concat_axi...  3.33 us
  transfers between devices with their start and end apart: 1, of which 1 were waited for; matrix products, arithmetic and copies ran while one was open for 2% of the time, Pallas kernels for 0%

profile of v1, /device:TPU:0, one launch (start us, length us, event | category | flops | bytes accessed | tf_op | source)
XLA Modules:
  0.0 102.5 jit_solution(7274149955971565520)
XLA Ops:
  0.0 0.0 copy-start
  0.0 0.8 scatter.7
  0.8 0.7 scatter.8.m_ref
  1.5 0.0 copy-start.3
  1.5 86.6 %shard_map.82 = bf16[2,256,512]{2,1,0:T(8,128)(2,1)} custom-call(s32[8,128]{1,0:T(8,128)} %scatter.8.m_ref, bf16[6,4096,128]{2,1,0:T(8,128)(2,1)} %bitcast.75, bf16[2,3,2048,512]{3,2,1,0:T(8,128)(2,1)} %bitcast.74), custom_call_target="tpu_custom_call" | custom-call | tf_op jit(solution)/shard_map/pallas_call | solution.py:259
  88.0 0.0 copy-start.1
  88.1 0.0 copy-start.2
  88.1 1.1 %fusion.21 = (bf16[1,256,512]{2,1,0:T(8,128)(2,1)S(1)}, bf16[1,256,512]{2,1,0:T(8,128)(2,1)S(1)}) fusion(bf16[2,256,512]{2,1,0:T(8,128)(2,1)} %shard_map.82), kind=kLoop, calls=%fused_computation.36 | loop fusion | bytes 1048576 | tf_op jit(solution)/shard_map/slice | solution.py:303
  89.2 0.0 copy-done.3
  89.2 0.1 iota_compare_fusion
  89.3 0.1 maximum_bitcast_fusion
  89.4 1.7 %fusion.2 = bf16[2,2,1,256,128]{3,4,0,1,2:T(8,128)(2,1)S(1)} fusion(bf16[1,2,2,128,512]{4,3,1,0,2:T(8,128)(2,1)S(1)} %get-tuple-element.22, bf16[1,2,2,128,512]{4,3,1,0,2:T(8,128)(2,1)S(1)} %get-tuple-element.21, bf16[1,2,2,256,512]{4,3,2,1,0:T(8,128)(2,1)} %param.12, pred[2,256]{1,0:T(4,128)(4,1)S(1)} %iota_compare_fusion), kind=kOutput, calls=%fused_computation.4 | convolution fusion | flops 269221888 | bytes 2359808 | tf_op jit(solution)/shard_map/oqsrb,sqjb->osjr/dot_general | solution.py:305
  91.1 1.0 copy.21
  92.1 3.7 %all-to-all-start = ((bf16[2,2,1,256,128]{3,0,1,2,4:T(2,128)(2,1)}), bf16[2,2,1,256,128]{3,0,1,2,4:T(2,128)(2,1)S(1)}, u32[]{:S(2)}, u32[]{:S(2)}) async-start(bf16[2,2,1,256,128]{3,0,1,2,4:T(2,128)(2,1)} %copy.21), calls=%async_computation | async-start | bytes 524288 | tf_op jit(solution)/shard_map/all_to_all | solution.py:311
  95.8 0.0 copy-done.1
  95.8 0.0 copy-done
  95.8 1.9 %gather_fusion = bf16[256,2,4,256]{3,2,1,0:T(4,128)(2,1)S(1)} fusion(bf16[2,2,256,4,256]{4,3,2,1,0:T(4,128)(2,1)S(1)} %copy-done, s32[256]{0:T(256)S(1)} %fusion.16), kind=kCustom, calls=%fused_computation | custom fusion | bytes 2099200 | tf_op jit(solution)/shard_map/vmap(jit(_take))/gather | solution.py:297
  97.7 0.0 copy-done.2
  97.8 0.1 compare_and_fusion
  97.8 3.3 %all-to-all-done = bf16[2,2,1,256,128]{3,0,1,2,4:T(2,128)(2,1)S(1)} async-done(((bf16[2,2,1,256,128]{3,0,1,2,4:T(2,128)(2,1)}), bf16[2,2,1,256,128]{3,0,1,2,4:T(2,128)(2,1)S(1)}, u32[]{:S(2)}, u32[]{:S(2)}) %all-to-all-start) | async-done | bytes 262176 | tf_op jit(solution)/shard_map/all_to_all | solution.py:311
  101.3 1.3 %fusion.5 = bf16[2,2,128,32]{2,3,1,0:T(8,128)(2,1)} fusion(bf16[2,128,2,4,256]{4,3,2,1,0:T(4,128)(2,1)S(1)} %bitcast.80, pred[2,128]{1,0:T(4,128)(4,1)S(1)} %get-tuple-element.25, bf16[1,2,2,4,256,32]{4,5,1,3,0,2:T(8,128)(2,1)S(1)} %get-tuple-element.24, bf16[1,2,2,4,256,32]{4,5,1,3,0,2:T(8,128)(2,1)S(1)} %get-tuple-element.23, ...), kind=kOutput, calls=%fused_computation.8 | convolution fusion | flops 68714496 | bytes 1606144 | tf_op jit(solution)/shard_map/oqsfjr,sqifj->soir/dot_general | solution.py:315
  (6 shorter events, 0.2 us)
Async XLA Ops:
  0.0 95.8 %copy-start = (bf16[2,2,256,4,256]{4,3,2,1,0:T(4,128)(2,1)S(1)}, bf16[2,2,256,4,256]{4,3,2,1,0:T(4,128)(2,1)}, u32[]{:S(2)}) copy-start(bf16[2,2,256,4,256]{4,3,2,1,0:T(4,128)(2,1)} %param.13) | copy-start | bytes 6291460
  1.5 87.7 %copy-start.3 = (s32[2]{0:T(128)S(1)}, s32[2]{0:T(128)}, u32[]{:S(2)}) copy-start(s32[2]{0:T(128)} %param.15) | copy-start | bytes 28
  88.0 7.7 %copy-start.1 = (s32[2,128]{1,0:T(2,128)S(1)}, s32[2,128]{1,0:T(2,128)}, u32[]{:S(2)}) copy-start(s32[2,128]{1,0:T(2,128)} %param.16) | copy-start | bytes 3076
  88.1 9.7 %copy-start.2 = (s32[2]{0:T(128)S(1)}, s32[2]{0:T(128)}, u32[]{:S(2)}) copy-start(s32[2]{0:T(128)} %param.17) | copy-start | bytes 28
  92.1 9.1 %all-to-all-start = ((bf16[2,2,1,256,128]{3,0,1,2,4:T(2,128)(2,1)}), bf16[2,2,1,256,128]{3,0,1,2,4:T(2,128)(2,1)S(1)}, u32[]{:S(2)}, u32[]{:S(2)}) async-start(bf16[2,2,1,256,128]{3,0,1,2,4:T(2,128)(2,1)} %copy.21), calls=%async_computation | async-start | bytes 524288 | tf_op jit(solution)/shard_map/all_to_all | solution.py:311

commit v2 on v1

--- a/solution.py
+++ b/solution.py
@@ -134,10 +134,23 @@
             device_id={"ma": peer}, device_id_type=MESH,
         )
 
-    def ship(ch):
-        @pl.loop(0, lanes - 1)
+    half = lanes // 2
+    quarter = (4 * me) // lanes
+    at_end = (quarter == 0) | (quarter == 3)
+
+    def ship_across(ch):
+        @pl.loop(0, lanes - half)
         def _(i):
             slab(ch, partner(me, lanes - 1 - i, lanes), me).start()
+
+    def ship(ch):
+        @pl.when(jnp.logical_not(at_end))
+        def _():
+            ship_across(ch)
+
+        @pl.loop(0, half - 1)
+        def _(i):
+            slab(ch, partner(me, half - 1 - i, lanes), me).start()
 
     pack(0)
     ship(0)
@@ -168,6 +181,12 @@
     def _(ch):
         pack(ch)
         ship(ch)
+
+    @pl.when(at_end)
+    def _():
+        @pl.loop(0, chunks)
+        def _(ch):
+            ship_across(ch)
 
     acc_r[...] = jnp.zeros_like(acc_r)
     acc_i[...] = jnp.zeros_like(acc_i)
@@ -249,9 +268,7 @@
     total, bases = beam.shape[2], beam.shape[3]
     chunks = parts * pols
     block, kblock = 32, 512
-    m_tile = jnp.zeros((8, 128), jnp.int32).at[:2].set(
-        jnp.broadcast_to(m_values[:, None], (2, 128))
-    )
+    m_tile = jnp.broadcast_to(jnp.tile(m_values, 4)[:, None], (8, 128))
     flat = sky.reshape(chunks, rows * slots, reals)
     any_space = pl.BlockSpec(memory_space=pl.ANY)
     vmem = pl.BlockSpec(memory_space=pltpu.VMEM)

time: 103 us -> 103 us (level)
    scatter x2 -> x0, local copies, waits for them, and re-layouts: 1.47 us -> none  [exchange(): jnp.zeros((8, 128), jnp.int32).at[:2]]
where the time goes in v2:
time: 103 us
  Pallas kernels  86.7 us (84%)
  local copies, waits for them, and re-layouts  5.62 us (5%)
  starting transfers between devices  3.72 us (4%)
  waiting for transfers between devices  3.33 us (3%)
  matrix products  2.97 us (3%)
    pallas_call x1, Pallas kernels, exchange(): pl.pallas_call(functools.partial(exchange_kernel, lanes, rows, slots, blo...  86.7 us
    all_to_all x1, starting transfers between devices, shards(): lax.all_to_all(coefficients[:, :, None], 'freq', split_axis=4, concat_axi...  3.72 us
    all_to_all x1, waiting for transfers between devices, shards(): lax.all_to_all(coefficients[:, :, None], 'freq', split_axis=4, concat_axi...  3.33 us
  transfers between devices with their start and end apart: 1, of which 1 were waited for; matrix products, arithmetic and copies ran while one was open for 2% of the time, Pallas kernels for 0%

profile of v2, /device:TPU:0, one launch (start us, length us, event | category | flops | bytes accessed | tf_op | source)
XLA Modules:
  0.0 102.8 jit_solution(1186140316709401080)
XLA Ops:
  0.0 0.0 copy-start
  0.0 0.8 tile.2
  0.8 0.1 broadcast_in_dim.57
  0.9 0.7 broadcast_in_dim.58.m_ref
  1.6 0.0 copy-start.3
  1.6 86.7 %shard_map.82 = bf16[2,256,512]{2,1,0:T(8,128)(2,1)} custom-call(s32[8,128]{1,0:T(8,128)} %broadcast_in_dim.58.m_ref, bf16[6,4096,128]{2,1,0:T(8,128)(2,1)} %bitcast.75, bf16[2,3,2048,512]{3,2,1,0:T(8,128)(2,1)} %bitcast.74), custom_call_target="tpu_custom_call" | custom-call | tf_op jit(solution)/shard_map/pallas_call | solution.py:276
  88.3 0.0 copy-start.1
  88.3 0.0 copy-start.2
  88.3 1.1 %fusion.21 = (bf16[1,256,512]{2,1,0:T(8,128)(2,1)S(1)}, bf16[1,256,512]{2,1,0:T(8,128)(2,1)S(1)}) fusion(bf16[2,256,512]{2,1,0:T(8,128)(2,1)} %shard_map.82), kind=kLoop, calls=%fused_computation.36 | loop fusion | bytes 1048576 | tf_op jit(solution)/shard_map/slice | solution.py:320
  89.5 0.0 copy-done.3
  89.5 0.1 iota_compare_fusion
  89.5 0.1 maximum_bitcast_fusion
  89.6 1.7 %fusion.2 = bf16[2,2,1,256,128]{3,4,0,1,2:T(8,128)(2,1)S(1)} fusion(bf16[1,2,2,128,512]{4,3,1,0,2:T(8,128)(2,1)S(1)} %get-tuple-element.10, bf16[1,2,2,128,512]{4,3,1,0,2:T(8,128)(2,1)S(1)} %get-tuple-element.9, bf16[1,2,2,256,512]{4,3,2,1,0:T(8,128)(2,1)} %param.10, pred[2,256]{1,0:T(4,128)(4,1)S(1)} %iota_compare_fusion), kind=kOutput, calls=%fused_computation.4 | convolution fusion | flops 269221888 | bytes 2359808 | tf_op jit(solution)/shard_map/oqsrb,sqjb->osjr/dot_general | solution.py:322
  91.3 1.0 copy.28
  92.3 3.7 %all-to-all-start = ((bf16[2,2,1,256,128]{3,0,1,2,4:T(2,128)(2,1)}), bf16[2,2,1,256,128]{3,0,1,2,4:T(2,128)(2,1)S(1)}, u32[]{:S(2)}, u32[]{:S(2)}) async-start(bf16[2,2,1,256,128]{3,0,1,2,4:T(2,128)(2,1)} %copy.28), calls=%async_computation | async-start | bytes 524288 | tf_op jit(solution)/shard_map/all_to_all | solution.py:328
  96.0 0.0 copy-done.1
  96.1 0.0 copy-done
  96.1 1.9 %gather_fusion = bf16[256,2,4,256]{3,2,1,0:T(4,128)(2,1)S(1)} fusion(bf16[2,2,256,4,256]{4,3,2,1,0:T(4,128)(2,1)S(1)} %copy-done, s32[256]{0:T(256)S(1)} %fusion.16), kind=kCustom, calls=%fused_computation | custom fusion | bytes 2099200 | tf_op jit(solution)/shard_map/vmap(jit(_take))/gather | solution.py:314
  98.0 0.0 copy-done.2
  98.0 0.1 compare_and_fusion
  98.1 3.3 %all-to-all-done = bf16[2,2,1,256,128]{3,0,1,2,4:T(2,128)(2,1)S(1)} async-done(((bf16[2,2,1,256,128]{3,0,1,2,4:T(2,128)(2,1)}), bf16[2,2,1,256,128]{3,0,1,2,4:T(2,128)(2,1)S(1)}, u32[]{:S(2)}, u32[]{:S(2)}) %all-to-all-start) | async-done | bytes 262176 | tf_op jit(solution)/shard_map/all_to_all | solution.py:328
  101.5 1.3 %fusion.5 = bf16[2,2,128,32]{2,3,1,0:T(8,128)(2,1)} fusion(bf16[2,128,2,4,256]{4,3,2,1,0:T(4,128)(2,1)S(1)} %bitcast.80, pred[2,128]{1,0:T(4,128)(4,1)S(1)} %get-tuple-element.13, bf16[1,2,2,4,256,32]{4,5,1,3,0,2:T(8,128)(2,1)S(1)} %get-tuple-element.12, bf16[1,2,2,4,256,32]{4,5,1,3,0,2:T(8,128)(2,1)S(1)} %get-tuple-element.11, ...), kind=kOutput, calls=%fused_computation.8 | convolution fusion | flops 68714496 | bytes 1606144 | tf_op jit(solution)/shard_map/oqsfjr,sqifj->soir/dot_general | solution.py:332
  (6 shorter events, 0.2 us)
Async XLA Ops:
  0.0 96.1 %copy-start = (bf16[2,2,256,4,256]{4,3,2,1,0:T(4,128)(2,1)S(1)}, bf16[2,2,256,4,256]{4,3,2,1,0:T(4,128)(2,1)}, u32[]{:S(2)}) copy-start(bf16[2,2,256,4,256]{4,3,2,1,0:T(4,128)(2,1)} %param.11) | copy-start | bytes 6291460
  1.6 87.9 %copy-start.3 = (s32[2]{0:T(128)S(1)}, s32[2]{0:T(128)}, u32[]{:S(2)}) copy-start(s32[2]{0:T(128)} %param.13) | copy-start | bytes 28
  88.3 7.7 %copy-start.1 = (s32[2,128]{1,0:T(2,128)S(1)}, s32[2,128]{1,0:T(2,128)}, u32[]{:S(2)}) copy-start(s32[2,128]{1,0:T(2,128)} %param.14) | copy-start | bytes 3076
  88.3 9.7 %copy-start.2 = (s32[2]{0:T(128)S(1)}, s32[2]{0:T(128)}, u32[]{:S(2)}) copy-start(s32[2]{0:T(128)} %param.15) | copy-start | bytes 28
  92.3 9.1 %all-to-all-start = ((bf16[2,2,1,256,128]{3,0,1,2,4:T(2,128)(2,1)}), bf16[2,2,1,256,128]{3,0,1,2,4:T(2,128)(2,1)S(1)}, u32[]{:S(2)}, u32[]{:S(2)}) async-start(bf16[2,2,1,256,128]{3,0,1,2,4:T(2,128)(2,1)} %copy.28), calls=%async_computation | async-start | bytes 524288 | tf_op jit(solution)/shard_map/all_to_all | solution.py:328

commit v3 on v1

--- a/solution.py
+++ b/solution.py
@@ -23,10 +23,12 @@
 
 def exchange_kernel(
     lanes, rows, slots, block, kblock,
-    m_ref, sky_ref, beam_ref, vis_ref,
+    m_ref, svd_count, kl_count, index_ref, sky_ref, beam_ref, svd_ref, kl_ref, out_ref,
     m_all, m_smem, sky_buf, wide, send, recv, extra_send, extra_recv, beam_buf,
     stage, mixed, turned, acc_r, acc_i,
+    svd_buf, kl_buf, chosen, coef_send, coef_recv,
     m_send, m_recv, m_local, sky_sem, beam_sem, send_sem, recv_sem, ex_send, ex_recv,
+    basis_sem, coef_sem, coef_arrived,
 ):
     me = lax.axis_index("ma")
     chunks = sky_ref.shape[0]
@@ -42,6 +44,14 @@
                 beam_ref.at[part, pol], beam_buf.at[part, pol], beam_sem.at[part, pol]
             ).start()
 
+    svd_load = pltpu.make_async_copy(svd_ref, svd_buf, basis_sem.at[0])
+    kl_load = pltpu.make_async_copy(kl_ref, kl_buf, basis_sem.at[1])
+    svd_load.start()
+    kl_load.start()
+    mine = lax.axis_index("freq")
+    bands = coef_send.shape[0]
+    share = coef_send.shape[3]
+
     barrier = pltpu.get_barrier_semaphore()
 
     @pl.loop(1, lanes)
@@ -50,7 +60,13 @@
             barrier, inc=1, device_id={"ma": partner(me, step, lanes)}, device_id_type=MESH
         )
 
-    pl.semaphore_wait(barrier, lanes - 1)
+    @pl.loop(1, bands)
+    def _(step):
+        pl.semaphore_signal(
+            barrier, inc=1, device_id={"freq": partner(mine, step, bands)}, device_id_type=MESH
+        )
+
+    pl.semaphore_wait(barrier, lanes - 1 + bands - 1)
 
     def m_copy(step):
         peer = partner(me, step, lanes)
@@ -168,6 +184,20 @@
     def _(ch):
         pack(ch)
         ship(ch)
+
+    svd_load.wait()
+    kl_load.wait()
+    modes, kept = kl_buf.shape[2], index_ref.shape[1]
+    for slot in range(2):
+        column = lax.broadcasted_iota(jnp.int32, (modes, kept), 0)
+        place = lax.broadcasted_iota(jnp.int32, (modes, kept), 1)
+        hit = (column == index_ref[pl.ds(slot, 1), :]) & (place < kl_count[slot])
+        pick = jnp.where(hit, 1.0, 0.0).astype(F32).T.astype(BF16)
+        for part in range(2):
+            for band in range(bands):
+                chosen[slot, part, band] = jnp.dot(
+                    pick, kl_buf[slot, part, :, band, :], preferred_element_type=F32
+                ).astype(BF16)
 
     acc_r[...] = jnp.zeros_like(acc_r)
     acc_i[...] = jnp.zeros_like(acc_i)
@@ -239,27 +269,69 @@
                 both, beam_buf[1 - part, pol, pl.ds(at, kblock), :], preferred_element_type=F32
             )
 
-    vis_ref[0] = acc_r[...].astype(BF16)
-    vis_ref[1] = acc_i[...].astype(BF16)
-
-
-def exchange(sky, beam, m_values):
-    lanes = lax.axis_size("ma")
+    def nt(left, right):
+        return lax.dot_general(left, right, (((1,), (1,)), ((), ())), preferred_element_type=F32)
+
+    modes_all = svd_buf.shape[2]
+    for slot in range(2):
+        vr = acc_r[pl.ds(slot * reals, reals), :].astype(BF16)
+        vi = acc_i[pl.ds(slot * reals, reals), :].astype(BF16)
+        ur, ui = svd_buf[slot, 0], svd_buf[slot, 1]
+        keep = lax.broadcasted_iota(jnp.int32, (reals, modes_all), 1) < svd_count[slot]
+        real = jnp.where(keep, nt(vr, ur) + nt(vi, ui), 0.0).astype(BF16)
+        imag = jnp.where(keep, nt(vi, ur) - nt(vr, ui), 0.0).astype(BF16)
+        for band in range(bands):
+            coef_send[band, 0, slot] = real[band * share:(band + 1) * share]
+            coef_send[band, 1, slot] = imag[band * share:(band + 1) * share]
+
+    def coef_copy(peer, sender):
+        return pltpu.make_async_remote_copy(
+            src_ref=coef_send.at[peer], dst_ref=coef_recv.at[sender],
+            send_sem=coef_sem.at[peer], recv_sem=coef_arrived.at[sender],
+            device_id={"freq": peer}, device_id_type=MESH,
+        )
+
+    @pl.loop(0, bands - 1)
+    def _(i):
+        coef_copy(partner(mine, bands - 1 - i, bands), mine).start()
+
+    coef_recv[mine] = coef_send[mine]
+
+    @pl.loop(1, bands)
+    def _(step):
+        peer = partner(mine, step, bands)
+        coef_copy(peer, peer).wait_recv()
+        coef_copy(peer, peer).wait_send()
+
+    for slot in range(2):
+        real = jnp.zeros((kept, share), F32)
+        imag = jnp.zeros((kept, share), F32)
+        for band in range(bands):
+            kr, ki = chosen[slot, 0, band], chosen[slot, 1, band]
+            sr, si = coef_recv[band, 0, slot], coef_recv[band, 1, slot]
+            real = real + nt(kr, sr) - nt(ki, si)
+            imag = imag + nt(kr, si) + nt(ki, sr)
+        out_ref[slot, 0] = real.astype(BF16)
+        out_ref[slot, 1] = imag.astype(BF16)
+
+
+def exchange(sky, beam, svd, kl, m_values, svd_count, kl_index, kl_count):
+    lanes, bands = lax.axis_size("ma"), lax.axis_size("freq")
+    kept, share = kl_index.shape[1], sky.shape[-1] // bands
     parts, pols, rows, slots, reals = sky.shape
     total, bases = beam.shape[2], beam.shape[3]
     chunks = parts * pols
     block, kblock = 32, 512
-    m_tile = jnp.zeros((8, 128), jnp.int32).at[:2].set(
-        jnp.broadcast_to(m_values[:, None], (2, 128))
-    )
+    m_tile = jnp.broadcast_to(jnp.tile(m_values, 4)[:, None], (8, 128))
     flat = sky.reshape(chunks, rows * slots, reals)
     any_space = pl.BlockSpec(memory_space=pl.ANY)
     vmem = pl.BlockSpec(memory_space=pltpu.VMEM)
+    smem = pl.BlockSpec(memory_space=pltpu.SMEM)
     dma = pltpu.SemaphoreType.DMA
     return pl.pallas_call(
         functools.partial(exchange_kernel, lanes, rows, slots, block, kblock),
-        out_shape=jax.ShapeDtypeStruct((2, 2 * reals, bases), BF16),
-        in_specs=[vmem, any_space, any_space],
+        out_shape=jax.ShapeDtypeStruct((2, 2, kept, share), BF16),
+        in_specs=[vmem, smem, smem, vmem, any_space, any_space, any_space, any_space],
         out_specs=vmem,
         scratch_shapes=[
             pltpu.VMEM((lanes, 8, 128), jnp.int32),
@@ -276,45 +348,27 @@
             pltpu.VMEM((2 * reals, kblock), BF16),
             pltpu.VMEM((2 * reals, bases), F32),
             pltpu.VMEM((2 * reals, bases), F32),
+            pltpu.VMEM(svd.shape, BF16),
+            pltpu.VMEM(kl.shape, BF16),
+            pltpu.VMEM((2, 2, bands, kept, svd.shape[2]), BF16),
+            pltpu.VMEM((bands, 2, 2, share, svd.shape[2]), BF16),
+            pltpu.VMEM((bands, 2, 2, share, svd.shape[2]), BF16),
             dma((lanes,)), dma((lanes,)), dma,
             dma((chunks,)), dma((2, pols)),
             dma((chunks, lanes)), dma((chunks, lanes)), dma((lanes,)), dma((lanes,)),
+            dma((2,)), dma((bands,)), dma((bands,)),
         ],
         compiler_params=pltpu.CompilerParams(
             collective_id=0, has_side_effects=True, vmem_limit_bytes=64_000_000
         ),
-    )(m_tile, flat, beam)
-
-
-def complex_stack(first_part, second_part):
-    return jnp.stack([jnp.stack([first_part, -second_part]), jnp.stack([second_part, first_part])])
+    )(m_tile, svd_count, kl_count, kl_index, flat, beam, svd, kl)
 
 
 def shards(sky_coeffs, beam_transfer, svd_basis, kl_basis, m_values, svd_count, kl_index, kl_count):
-    svd_owner = svd_basis[0]
-    mode_total = svd_owner.shape[2]
-    reals = sky_coeffs.shape[-1]
-    selected = jax.vmap(lambda basis_one, chosen: jnp.take(basis_one, chosen, axis=1))(
-        kl_basis, kl_index
+    return exchange(
+        sky_coeffs[0, :, :, :, 0], beam_transfer[0, 0], svd_basis[0], kl_basis,
+        m_values, svd_count, kl_index, kl_count,
     )
-    visibility = exchange(sky_coeffs[0, :, :, :, 0], beam_transfer[0, 0], m_values)
-    visibility = visibility.reshape(2, 2, reals, visibility.shape[-1])
-    rotated = jnp.stack(
-        [jnp.stack([visibility[0], visibility[1]]), jnp.stack([visibility[1], -visibility[0]])]
-    )
-    coefficients = jnp.einsum(
-        "oqsrb,sqjb->osjr", rotated, svd_owner, preferred_element_type=jnp.float32
-    )
-    mode_mask = jnp.arange(mode_total, dtype=jnp.int32)[None, :] < svd_count[:, None]
-    coefficients = jnp.where(mode_mask[None, :, :, None], coefficients, 0.0).astype(jnp.bfloat16)
-    keep_mask = jnp.arange(selected.shape[2], dtype=jnp.int32)[None, :] < kl_count[:, None]
-    spread = lax.all_to_all(
-        coefficients[:, :, None], "freq", split_axis=4, concat_axis=2, tiled=True
-    )
-    stacked = complex_stack(spread[0], spread[1])
-    kl_out = jnp.einsum("oqsfjr,sqifj->soir", stacked, selected, preferred_element_type=jnp.float32)
-    kl_out = jnp.where(keep_mask[:, None, :, None], kl_out, 0.0)
-    return kl_out.astype(jnp.bfloat16)
 
 
 def solution(mesh):

time: 103 us -> 96.2 us (0.934)
  Pallas kernels: 86.6 us -> 93 us
  starting transfers between devices: 3.72 us -> 0 us
  waiting for transfers between devices: 3.33 us -> 0 us
  matrix products: 2.97 us -> 0 us
  local copies, waits for them, and re-layouts: 5.54 us -> 3.01 us
    pallas_call x1, Pallas kernels: 86.6 us -> 93 us  [exchange(): pl.pallas_call(functools.partial(exchange_kernel, lanes, rows, slots, blo...]
    all_to_all x1 -> x0, starting transfers between devices: 3.72 us -> none  [shards(): lax.all_to_all(coefficients[:, :, None], 'freq', split_axis=4, concat_axi...]
    all_to_all x1 -> x0, waiting for transfers between devices: 3.33 us -> none  [shards(): lax.all_to_all(coefficients[:, :, None], 'freq', split_axis=4, concat_axi...]
    dot_general x2 -> x0, matrix products: 2.97 us -> none  [the longest x1 1.71 us: shards(): jnp.einsum('oqsrb,sqjb->osjr', rotated, svd_owner, preferred_element_type...]
    gather x1 -> x0, local copies, waits for them, and re-layouts: 1.93 us -> none  [shards(): jnp.take(basis_one, chosen, axis=1)]
    pallas_call x0 -> x1, local copies, waits for them, and re-layouts: none -> 1.6 us  [exchange(): pl.pallas_call(functools.partial(exchange_kernel, lanes, rows, slots, blo...]
    scatter x2 -> x0, local copies, waits for them, and re-layouts: 1.47 us -> none  [exchange(): jnp.zeros((8, 128), jnp.int32).at[:2]]
    slice x1 -> x0, local copies, waits for them, and re-layouts: 1.08 us -> none  [shards(): visibility[1]]
  transfers between devices with their start and end apart: 1 -> 0, of which waited for: 1 -> 0; matrix products, arithmetic and copies ran while one was open for 2% -> 0% of each run, Pallas kernels for 0% -> 0%
where the time goes in v3:
time: 96.2 us; the launch traced here: 96 us
  Pallas kernels  93 us (97%)
  local copies, waits for them, and re-layouts  3.01 us (3%)
    pallas_call x1, Pallas kernels, exchange(): pl.pallas_call(functools.partial(exchange_kernel, lanes, rows, slots, blo...  93 us

profile of v3, /device:TPU:0, one launch (start us, length us, event | category | flops | bytes accessed | tf_op | source)
XLA Modules:
  0.0 96.0 jit_solution(16063101395817253456)
XLA Ops:
  0.0 0.7 tile.2
  0.7 0.1 broadcast_in_dim.7
  0.7 0.7 broadcast_in_dim.8.m_ref
  1.4 93.0 %shard_map.82 = bf16[2,2,128,32]{3,2,1,0:T(8,128)(2,1)} custom-call(s32[8,128]{1,0:T(8,128)} %broadcast_in_dim.8.m_ref, s32[2]{0:T(128)} %svd_count.1, s32[2]{0:T(128)} %kl_count.1, s32[2,128]{1,0:T(2,128)} %index_ref.1, bf16[6,4096,128]{2,1,0:T(8,128)(2,1)} %bitcast.4, bf16[2,3,2048,512]{3,2,1,0:T(8,128)(2,1)} %bitcast.3, bf16[2,2,256,512]{3,2,1,0:T(8,128)(2,1)} %bitcast.5, ...), custom_call_target="tpu_custom_call" | custom-call | tf_op jit(solution)/shard_map/pallas_call | solution.py:331
  94.4 1.6 %copy.10 = bf16[2,2,128,32]{2,3,1,0:T(8,128)(2,1)} copy(bf16[2,2,128,32]{3,2,1,0:T(8,128)(2,1)} %shard_map.82) | data formatting | bytes 65536 | tf_op jit(solution)/shard_map/pallas_call | solution.py:331

commit v4 on v3

--- a/solution.py
+++ b/solution.py
@@ -25,7 +25,7 @@
     lanes, rows, slots, block, kblock,
     m_ref, svd_count, kl_count, index_ref, sky_ref, beam_ref, svd_ref, kl_ref, out_ref,
     m_all, m_smem, sky_buf, wide, send, recv, extra_send, extra_recv, beam_buf,
-    stage, mixed, turned, acc_r, acc_i,
+    stage, mixed, acc_r, acc_i,
     svd_buf, kl_buf, chosen, coef_send, coef_recv,
     m_send, m_recv, m_local, sky_sem, beam_sem, send_sem, recv_sem, ex_send, ex_recv,
     basis_sem, coef_sem, coef_arrived,
@@ -123,7 +123,7 @@
             first1 = (excess - me + lanes - 1) // lanes
             residue = lanes * first0 + me - m0
 
-            @pl.loop(0, rows // block)
+            @pl.loop(0, rows // block, unroll=True)
             def _(i):
                 k0 = i * block
                 r0 = jnp.clip(first0 + k0, 0, rows)
@@ -237,7 +237,7 @@
             spare_all = extra_recv[lane1].astype(F32)
             spare = jnp.sum(jnp.where(tile == ch, spare_all, 0.0), axis=0, keepdims=True)
 
-            @pl.loop(0, rows // block)
+            @pl.loop(0, rows // block, unroll=True)
             def _(i):
                 k0 = pl.multiple_of(i * block, block)
                 v0 = stage[lane0, pl.ds(k0, block), :]
@@ -254,14 +254,14 @@
         pol = ch % pols
         sign = (1 - 2 * part).astype(F32)
 
-        @pl.loop(0, total // kblock)
+        @pl.loop(0, total // kblock, unroll=True)
         def _(i):
             at = pl.multiple_of(i * kblock, kblock)
             flat = mixed[pl.ds(at, kblock), :].T
             place = lax.broadcasted_iota(jnp.int32, (reals, kblock), 1) + at
-            turned[pl.ds(0, reals), :] = jnp.where(place < start1, flat, 0.0).astype(BF16)
-            turned[pl.ds(reals, reals), :] = jnp.where(place < start1, 0.0, flat).astype(BF16)
-            both = turned[...]
+            both = jnp.concatenate(
+                [jnp.where(place < start1, flat, 0.0), jnp.where(place < start1, 0.0, flat)], axis=0
+            ).astype(BF16)
             acc_r[...] += sign * jnp.dot(
                 both, beam_buf[part, pol, pl.ds(at, kblock), :], preferred_element_type=F32
             )
@@ -345,7 +345,6 @@
             pltpu.VMEM((2, pols, total, bases), BF16),
             pltpu.VMEM((lanes, rows, reals), F32),
             pltpu.VMEM((total, reals), F32),
-            pltpu.VMEM((2 * reals, kblock), BF16),
             pltpu.VMEM((2 * reals, bases), F32),
             pltpu.VMEM((2 * reals, bases), F32),
             pltpu.VMEM(svd.shape, BF16),

time: 96.2 us -> 94.8 us (0.985)
  Pallas kernels: 93 us -> 91.6 us
    pallas_call x1, Pallas kernels: 93 us -> 91.6 us  [exchange(): pl.pallas_call(functools.partial(exchange_kernel, lanes, rows, slots, blo...]
where the time goes in v4:
time: 94.8 us; the launch traced here: 94.7 us
  Pallas kernels  91.6 us (97%)
  local copies, waits for them, and re-layouts  3.01 us (3%)
    pallas_call x1, Pallas kernels, exchange(): pl.pallas_call(functools.partial(exchange_kernel, lanes, rows, slots, blo...  91.6 us

profile of v4, /device:TPU:0, one launch (start us, length us, event | category | flops | bytes accessed | tf_op | source)
XLA Modules:
  0.0 94.7 jit_solution(17108854571639941070)
XLA Ops:
  0.0 0.7 tile.2
  0.7 0.1 broadcast_in_dim.7
  0.7 0.7 broadcast_in_dim.8.m_ref
  1.4 91.6 %shard_map.82 = bf16[2,2,128,32]{3,2,1,0:T(8,128)(2,1)} custom-call(s32[8,128]{1,0:T(8,128)} %broadcast_in_dim.8.m_ref, s32[2]{0:T(128)} %svd_count.1, s32[2]{0:T(128)} %kl_count.1, s32[2,128]{1,0:T(2,128)} %index_ref.1, bf16[6,4096,128]{2,1,0:T(8,128)(2,1)} %bitcast.4, bf16[2,3,2048,512]{3,2,1,0:T(8,128)(2,1)} %bitcast.3, bf16[2,2,256,512]{3,2,1,0:T(8,128)(2,1)} %bitcast.5, ...), custom_call_target="tpu_custom_call" | custom-call | tf_op jit(solution)/shard_map/pallas_call | solution.py:331
  93.1 1.6 %copy.10 = bf16[2,2,128,32]{2,3,1,0:T(8,128)(2,1)} copy(bf16[2,2,128,32]{3,2,1,0:T(8,128)(2,1)} %shard_map.82) | data formatting | bytes 65536 | tf_op jit(solution)/shard_map/pallas_call | solution.py:331
